TPU v7x, 32 devices: a whole 2x2x4 slice. The times are simulated.
32 devices in a mesh: section: 2 (over core), ctx: 4 (over z), mp: 4 (over y, x).
Axes of the slice: x: 2, y: 2, z: 4, core: 2. Of those that a mesh axis runs over, the one named last changes fastest.
Arguments:
- frames: bfloat16 [2, 16, 128, 512], P('section', 'ctx'), may hold values from -6 to 6
- w_conv: bfloat16 [3, 512, 512], replicated, may hold values from -0.15625 to 0.15625
- w_lat: bfloat16 [512, 16], replicated, may hold values from -0.25 to 0.25
- dest: int32 [2, 512, 1], P(None, 'ctx'), may hold values from 0 to 3; in each aligned block of 128 rows (0 to 127, 128 to 255, ..., all dimensions but the last counted through in order) at most 48 rows name the same one
- pick: int32 [2, 512], P(None, 'ctx'), may hold values from 0 to 6
- w_embed: bfloat16 [64, 6144], replicated, may hold values from -0.75 to 0.75
- gain: float32 [6144], replicated, may hold values from 0.25 to 1.75
- w_qkv: bfloat16 [6144, 3, 4096], P(None, None, 'mp'), may hold values from -0.078125 to 0.078125
Outputs:
- attended: bfloat16 [2, 768, 4096], P('section', 'ctx', 'mp')
Inputs may be any that keep to these rules, and one draw needn't show every extreme that they name: `dest`: among the 128 rows of one frame block, at most 48 name the same context shard, and some frame block reaches 48.
All inputs are finite; a program needn't handle non-finite values.
Results may differ from a plain program's by a relative error of at most 0.0061.
Values may be sent and summed in bfloat16 or wider, within the bound.
A program may use at most 128 MiB of HBM per device.

v0:
```python
import jax
import jax.numpy as jnp
from jax import lax
from jax.sharding import PartitionSpec as P

HEAD = 128
GROUP = 4


def partner(block, axis, distance):
    count = lax.axis_size(axis)
    route = []
    for low in range(count):
        high = low | 1 << distance
        if high != low and high < count:
            route += [(low, high), (high, low)]
    return lax.ppermute(block, axis, route)


def encode(frame_block, w_conv, w_lat):
    frame_count = frame_block.shape[0]
    cells_here = frame_block.shape[1]
    channels = frame_block.shape[2]
    empty_frame = jnp.zeros_like(frame_block[:1])
    back_one = jnp.concatenate([empty_frame, frame_block[:-1]], axis=0)
    back_two = jnp.concatenate([empty_frame, empty_frame, frame_block[:-2]], axis=0)
    hidden = jnp.dot(
        frame_block.reshape(-1, channels), w_conv[0], preferred_element_type=jnp.float32
    )
    hidden = hidden + jnp.dot(
        back_one.reshape(-1, channels), w_conv[1], preferred_element_type=jnp.float32
    )
    hidden = hidden + jnp.dot(
        back_two.reshape(-1, channels), w_conv[2], preferred_element_type=jnp.float32
    )
    active = jax.nn.silu(hidden).astype(jnp.bfloat16)
    latent = jnp.dot(active, w_lat, preferred_element_type=jnp.float32).astype(jnp.bfloat16)
    return latent.reshape(frame_count, cells_here // 4, 4 * w_lat.shape[1])


def head_norm(values):
    return values * lax.rsqrt(jnp.mean(values * values, axis=-1, keepdims=True) + 1e-06)


def on_device(frames, w_conv, w_lat, dest, pick, w_embed, gain, w_qkv):
    frame_block = frames[0]
    patch_grid = encode(frame_block, w_conv, w_lat)
    patch_rows = patch_grid.reshape(-1, patch_grid.shape[-1])
    arrived = partner(patch_rows, "section", 0)
    shard_count = lax.axis_size("ctx")
    row_count = arrived.shape[0]
    source = 1 - lax.axis_index("section")
    targets = lax.dynamic_index_in_dim(dest[:, :, 0], source, 0, keepdims=False)
    choose = lax.dynamic_index_in_dim(pick, source, 0, keepdims=False)
    tier = (choose >= 4).astype(jnp.int32) + (choose >= 6).astype(jnp.int32)
    labels = targets // GROUP + shard_count // GROUP * tier + 1
    onehot = (targets[:, None] == jnp.arange(shard_count, dtype=jnp.int32)[None, :]).astype(
        jnp.int32
    )
    before = jnp.cumsum(onehot, axis=0, dtype=jnp.int32) - onehot
    within = jnp.sum(before * onehot, axis=1, dtype=jnp.int32)
    capacity = max(2, 3 * row_count // (2 * shard_count))
    position = targets * capacity + within
    outgoing = (
        jnp.zeros((shard_count * capacity, arrived.shape[1]), jnp.bfloat16)
        .at[position]
        .set(arrived)
    )
    outgoing = outgoing.reshape(shard_count, capacity, arrived.shape[1])
    out_labels = jnp.zeros((shard_count * capacity,), jnp.int32).at[position].set(labels)
    out_labels = out_labels.reshape(shard_count, capacity)
    incoming, in_labels = (
        lax.all_to_all(outgoing, "ctx", split_axis=0, concat_axis=0, tiled=True),
        lax.all_to_all(out_labels, "ctx", split_axis=0, concat_axis=0, tiled=True),
    )
    packed = incoming.reshape(-1, incoming.shape[-1])
    owners = in_labels.reshape(-1)
    embedded = jnp.dot(packed, w_embed, preferred_element_type=jnp.float32)
    normed = (
        embedded * lax.rsqrt(jnp.mean(embedded * embedded, axis=-1, keepdims=True) + 1e-06) * gain
    ).astype(jnp.bfloat16)
    heads_here = w_qkv.shape[2] // HEAD
    projected = jnp.dot(
        normed, w_qkv.reshape(w_qkv.shape[0], -1), preferred_element_type=jnp.float32
    )
    projected = projected.reshape(-1, 3, heads_here, HEAD)
    queries = head_norm(projected[:, 0]).astype(jnp.bfloat16)
    keys_own = head_norm(projected[:, 1]).astype(jnp.bfloat16)
    values_own = projected[:, 2].astype(jnp.bfloat16)
    factor = 1.0 / HEAD**0.5
    key_piece = lax.all_gather(keys_own, "ctx", axis=0, tiled=True)
    value_piece = lax.all_gather(values_own, "ctx", axis=0, tiled=True)
    label_piece = lax.all_gather(owners, "ctx", axis=0, tiled=True)
    scores = (
        jnp.einsum("qhd,khd->hqk", queries, key_piece, preferred_element_type=jnp.float32) * factor
    )
    allowed = (owners[:, None] == label_piece[None, :]) & (owners[:, None] > 0)
    expo = jnp.where(allowed[None], jnp.exp(scores), 0.0)
    total = jnp.sum(expo, axis=-1).T
    summed = jnp.einsum(
        "hqk,khd->qhd", expo.astype(jnp.bfloat16), value_piece, preferred_element_type=jnp.float32
    )
    summed, total = (summed, total)
    empty_slot = (owners == 0).astype(jnp.float32)
    attended = summed / (total + empty_slot[:, None])[:, :, None]
    return attended.reshape(1, queries.shape[0], heads_here * HEAD).astype(jnp.bfloat16)


def solution(mesh):
    in_specs = (
        P("section", "ctx", None, None),
        P(),
        P(),
        P(None, "ctx", None),
        P(None, "ctx"),
        P(),
        P(),
        P(None, None, "mp"),
    )
    out_specs = P("section", "ctx", "mp")
    return jax.shard_map(
        on_device, mesh=mesh, in_specs=in_specs, out_specs=out_specs, check_vma=False
    )
```

profile of v0, /device:TPU:0, one launch (start us, length us, event | category | flops | bytes accessed | tf_op | source)
XLA Modules:
  0.0 183.4 jit_solution(528463704101767966)
XLA Ops:
  6.5 1.2 slice_bitcast_fusion.2
  7.7 1.0 slice_bitcast_fusion.3
  8.7 0.8 concatenate.8
  9.6 1.6 fusion.31
  11.2 0.0 copy-done.2
  11.2 0.0 copy-start.3
  11.2 0.4 convolution_add_fusion.1
  11.7 1.8 convolution_convert_fusion
  13.5 0.1 copy.9
  13.6 0.1 reshape_reshape.3
  13.8 0.6 collective-permute-start
  14.3 0.1 fusion.40
  14.4 0.2 reduce_window_sum.11
  14.6 0.2 select_reduce_fusion
  14.8 0.4 collective-permute-done
  15.2 0.9 scatter_custom_fusion
  16.1 0.7 reshape.205
  16.8 6.2 %all-to-all-start = ((bf16[4,2,1536]{2,1,0:T(2,128)(2,1)}), bf16[4,2,1536]{2,1,0:T(2,128)(2,1)S(1)}, u32[]{:S(2)}, u32[]{:S(2)}) async-start(bf16[4,2,1536]{2,1,0:T(2,128)(2,1)} %reshape.205), calls=%async_computation | async-start | bytes 49152 | tf_op jit(solution)/shard_map/all_to_all | solution.py:73
  23.0 0.0 all-gather.4.cloned.1.call-start
  23.0 48.7 %copy.10 = bf16[6144,3,1024]{0,2,1:T(8,128)(2,1)} copy(bf16[6144,3,1024]{2,0,1:T(8,128)(2,1)} %param.15) | data formatting | bytes 75497472 | tf_op args[7]
  71.7 0.0 all-to-all-done
  71.7 0.1 reshape.206
  71.8 2.9 %multiply_reduce_fusion = (f32[192]{0:T(256)S(1)}, f32[192,6144]{1,0:T(8,128)}) fusion(bf16[192,64]{1,0:T(8,128)(2,1)S(1)} %bitcast.92, bf16[64,6144]{1,0:T(8,128)(2,1)S(1)} %copy-done), kind=kOutput, calls=%fused_computation.4 | convolution fusion | flops 153354048 | bytes 5530368 | tf_op jit(solution)/shard_map/dot_general | solution.py:78
  74.7 0.0 copy-start.7
  74.7 18.8 %fusion.5 = f32[192,3,8,128]{3,0,2,1:T(8,128)S(1)} fusion(bf16[3,8,128,6144]{3,2,1,0:T(8,128)(2,1)} %bitcast.88, f32[192,6144]{1,0:T(8,128)} %get-tuple-element.10, f32[6144]{0:T(1024)S(1)} %copy-done.5, f32[192]{0:T(256)S(1)} %add_rsqrt_fusion.2), kind=kOutput, calls=%fused_computation.9 | convolution fusion | flops 7251296256 | bytes 44851968 | tf_op jit(solution)/shard_map/dot_general | solution.py:83
  93.5 0.6 multiply_reduce_fusion.2
  94.2 1.0 multiply_convert_fusion.2
  95.2 0.0 all-gather.4.cloned.1.call-update
  95.2 0.0 all-gather.6.cloned.1.call-start
  95.3 0.8 slice.71
  96.1 0.0 all-gather.6.cloned.1.call-update
  96.1 1.0 scatter_custom_fusion.1
  97.1 0.7 all_to_all.10
  97.8 5.1 %all-to-all-start.1 = ((s32[4,1,48]{2,1,0:T(1,128)}), s32[4,1,48]{2,1,0:T(1,128)S(1)}, u32[]{:S(2)}, u32[]{:S(2)}) async-start(s32[4,1,48]{2,1,0:T(1,128)} %all_to_all.10), calls=%async_computation.1 | async-start | bytes 4096 | tf_op jit(solution)/shard_map/all_to_all | solution.py:74
  102.9 0.6 dynamic-slice.1
  104.1 4.3 %all-to-all-done.1 = s32[4,1,48]{2,1,0:T(1,128)S(1)} async-done(((s32[4,1,48]{2,1,0:T(1,128)}), s32[4,1,48]{2,1,0:T(1,128)S(1)}, u32[]{:S(2)}, u32[]{:S(2)}) %all-to-all-start.1) | async-done | bytes 800 | tf_op jit(solution)/shard_map/all_to_all | solution.py:74
  108.4 0.6 broadcast.155
  109.0 0.6 reduce.3
  109.6 0.1 reshape.186
  109.7 0.2 dynamic-update-slice
  109.9 7.0 %all-reduce.2 = s32[768]{0:T(1024)S(1)} all-reduce(s32[768]{0:T(1024)S(1)} %dynamic-update-slice), channel_id=1, replica_groups=mesh['section'=2,'ctx'=4,'mp'=4] {'ctx'}, use_global_device_ids=true, to_apply=%add.2 | all-reduce | flops 768 | bytes 6144
  116.9 0.2 compare_and_fusion
  117.1 16.9 %all-gather.4.cloned.1.call-done = bf16[768,8,128]{2,0,1:T(8,128)(2,1)} async-done(((bf16[192,8,128]{2,0,1:T(8,128)(2,1)}), bf16[768,8,128]{2,0,1:T(8,128)(2,1)}) %all-gather.4.cloned.1.call-update) | async-done | bytes 1572880 | tf_op jit(solution)/shard_map/all_gather | solution.py:91
  134.1 4.8 %fusion = (f32[8,192]{1,0:T(8,128)S(1)}, f32[8,192,768]{2,1,0:T(8,128)}) fusion(pred[192,768]{1,0:T(8,128)(4,1)S(1)} %compare_and_fusion, bf16[768,8,128]{2,0,1:T(8,128)(2,1)} %all-gather.4.cloned.1.call-done, f32[192,3,8,128]{3,0,2,1:T(8,128)S(1)} %fusion.5, f32[192,8]{0,1:T(8,128)S(1)} %add_rsqrt_fusion.1), kind=kOutput, calls=%fused_computation.5 | convolution fusion | flops 305920512 | bytes 7239680 | tf_op jit(solution)/shard_map/qhd,khd->hqk/dot_general | solution.py:95
  138.9 32.6 %all-gather.6.cloned.1.call-done = bf16[768,1,8,128]{3,0,2,1:T(8,128)(2,1)} async-done(((bf16[192,1,8,128]{3,0,2,1:T(8,128)(2,1)}), bf16[768,1,8,128]{3,0,2,1:T(8,128)(2,1)}) %all-gather.6.cloned.1.call-update) | async-done | bytes 1572880 | tf_op jit(solution)/shard_map/all_gather | solution.py:92
  171.5 3.8 %fusion.23 = bf16[192,8,128]{2,0,1:T(8,128)(2,1)S(1)} fusion(bf16[768,1,8,128]{3,0,2,1:T(8,128)(2,1)} %all-gather.6.cloned.1.call-done, f32[8,192,768]{2,1,0:T(8,128)} %get-tuple-element.12, pred[192,768]{1,0:T(8,128)(4,1)S(1)} %compare_and_fusion, f32[192,8]{0,1:T(8,128)S(1)} %add_bitcast_fusion), kind=kOutput, calls=%fused_computation.22 | convolution fusion | flops 305922048 | bytes 6838272 | tf_op jit(solution)/shard_map/hqk,khd->qhd/dot_general | solution.py:100
  175.4 0.3 copy.11
  175.6 0.9 convert_element_type.66
  (23 shorter events, 0.1 us)
Async XLA Ops:
  6.5 65.3 %copy-start = (bf16[64,6144]{1,0:T(8,128)(2,1)S(1)}, bf16[64,6144]{1,0:T(8,128)(2,1)}, u32[]{:S(2)}) copy-start(bf16[64,6144]{1,0:T(8,128)(2,1)} %param.13) | copy-start | bytes 2359300
  6.5 4.7 %copy-start.2 = (bf16[3,512,512]{2,1,0:T(8,128)(2,1)S(1)}, bf16[3,512,512]{2,1,0:T(8,128)(2,1)}, u32[]{:S(2)}) copy-start(bf16[3,512,512]{2,1,0:T(8,128)(2,1)} %param.9) | copy-start | bytes 4718596
  6.5 5.1 %copy-start.6 = (bf16[512,16]{0,1:T(8,128)(2,1)S(1)}, bf16[512,16]{0,1:T(8,128)(2,1)}, u32[]{:S(2)}) copy-start(bf16[512,16]{0,1:T(8,128)(2,1)} %param.10) | copy-start | bytes 49156
  11.2 3.1 %copy-start.3 = (s32[2,128,1]{1,2,0:T(1,128)S(1)}, s32[2,128,1]{1,2,0:T(1,128)}, u32[]{:S(2)}) copy-start(s32[2,128,1]{1,2,0:T(1,128)} %param.11) | copy-start | bytes 3076
  13.8 1.4 collective-permute-start
  16.8 54.9 %all-to-all-start = ((bf16[4,2,1536]{2,1,0:T(2,128)(2,1)}), bf16[4,2,1536]{2,1,0:T(2,128)(2,1)S(1)}, u32[]{:S(2)}, u32[]{:S(2)}) async-start(bf16[4,2,1536]{2,1,0:T(2,128)(2,1)} %reshape.205), calls=%async_computation | async-start | bytes 49152 | tf_op jit(solution)/shard_map/all_to_all | solution.py:73
  23.0 111.1 %all-gather.4.cloned.1.call-start = ((), (), s32[]{:S(2)}) async-start(), calls=%async_computation.2 | async-start | bytes 1966080 | tf_op jit(solution)/shard_map/all_gather | solution.py:91
  71.7 3.0 %copy-start.5 = (f32[6144]{0:T(1024)S(1)}, f32[6144]{0:T(1024)}, u32[]{:S(2)}) copy-start(f32[6144]{0:T(1024)} %param.14) | copy-start | bytes 73732
  74.7 21.4 %copy-start.4 = (s32[2,128]{1,0:T(2,128)S(1)}, s32[2,128]{1,0:T(2,128)}, u32[]{:S(2)}) copy-start(s32[2,128]{1,0:T(2,128)} %param.12) | copy-start | bytes 3076
  74.7 28.1 %copy-start.7 = (u32[32]{0:T(128)S(1)}, u32[32]{0:T(128)}, u32[]{:S(2)}) copy-start(u32[32]{0:T(128)} %constant.76) | copy-start | bytes 388
  95.2 76.3 %all-gather.6.cloned.1.call-start = ((), (), s32[]{:S(2)}) async-start(), calls=%async_computation.3 | async-start | bytes 1966080 | tf_op jit(solution)/shard_map/all_gather | solution.py:92
  97.8 10.6 %all-to-all-start.1 = ((s32[4,1,48]{2,1,0:T(1,128)}), s32[4,1,48]{2,1,0:T(1,128)S(1)}, u32[]{:S(2)}, u32[]{:S(2)}) async-start(s32[4,1,48]{2,1,0:T(1,128)} %all_to_all.10), calls=%async_computation.1 | async-start | bytes 4096 | tf_op jit(solution)/shard_map/all_to_all | solution.py:74
  171.5 5.0 %copy-start.1 = (bf16[64,6144]{1,0:T(8,128)(2,1)S(1)}, bf16[64,6144]{1,0:T(8,128)(2,1)}, u32[]{:S(2)}) copy-start(bf16[64,6144]{1,0:T(8,128)(2,1)} %param.13) | copy-start | bytes 2359300
Sparse Core Ops, SparseCore 0:
  95.3 38.6 all-gather.3
  135.6 35.8 all-gather.5
where the time goes:
time: 185 us; the launch traced here: 183 us
  local copies, waits for them, and re-layouts  58.8 us (32%)
  waiting for transfers between devices  54.3 us (29%)
  matrix products  34.2 us (18%)
  between operations  14.2 us (8%)
  starting transfers between devices  11.9 us (6%)
  blocking collectives  7.03 us (4%)
  other arithmetic  2.93 us (2%)
    unnamed x22, local copies, waits for them, and re-layouts  50.4 us
    all_gather x1, waiting for transfers between devices, on_device(): value_piece = lax.all_gather(values_own, 'ctx', axis=0, tiled=True)  32.6 us
    dot_general x1, matrix products, on_device(): jnp.dot(normed, w_qkv.reshape(w_qkv.shape[0], -1), preferred_element_type...  18.8 us
    all_gather x1, waiting for transfers between devices, on_device(): key_piece = lax.all_gather(keys_own, 'ctx', axis=0, tiled=True)  16.9 us
    unnamed x1, blocking collectives  7.03 us
    all_to_all x1, starting transfers between devices, on_device(): lax.all_to_all(outgoing, 'ctx', split_axis=0, concat_axis=0, tiled=True)  6.2 us
    all_to_all x1, starting transfers between devices, on_device(): lax.all_to_all(out_labels, 'ctx', split_axis=0, concat_axis=0, tiled=True)  5.09 us
    dot_general x1, matrix products, on_device(): jnp.einsum('qhd,khd->hqk', queries, key_piece, preferred_element_type=jnp...  4.84 us
  transfers between devices with their start and end apart: 5, of which 4 were waited for; matrix products, arithmetic and copies ran while one was open for 32% of the time, Pallas kernels for 0%

commit v1 on v0

--- a/solution.py
+++ b/solution.py
@@ -5,6 +5,32 @@
 
 HEAD = 128
 GROUP = 4
+
+
+def state_state(buf, axis_name, where_dim, local, ndim_at):
+    mixed_arr, b_now, out_arr = (
+        lax.psum(1, axis_name),
+        lax.axis_index(axis_name),
+        buf.shape[where_dim],
+    )
+    back = right_arr = buf
+    far_arr, w2 = ([], [])
+    for src_i in range(mixed_arr // 2 + 1):
+        far_arr.append(local(back, (b_now - src_i) % mixed_arr * out_arr))
+        if 0 < src_i < mixed_arr - mixed_arr // 2:
+            w2.append(local(right_arr, (b_now + src_i) % mixed_arr * out_arr))
+        back = lax.ppermute(
+            back, axis_name, list(map(lambda i: (i, (i + 1) % mixed_arr), range(mixed_arr)))
+        )
+        right_arr = lax.ppermute(
+            right_arr, axis_name, list(map(lambda i: (i, (i - 1) % mixed_arr), range(mixed_arr)))
+        )
+    current_arr = jnp.roll(
+        jnp.concatenate([*far_arr[::-1], *w2], axis=ndim_at),
+        shift=(b_now - mixed_arr // 2) * far_arr[0].shape[ndim_at],
+        axis=ndim_at,
+    )
+    return current_arr
 
 
 def partner(block, axis, distance):
@@ -88,11 +114,19 @@
     keys_own = head_norm(projected[:, 1]).astype(jnp.bfloat16)
     values_own = projected[:, 2].astype(jnp.bfloat16)
     factor = 1.0 / HEAD**0.5
-    key_piece = lax.all_gather(keys_own, "ctx", axis=0, tiled=True)
     value_piece = lax.all_gather(values_own, "ctx", axis=0, tiled=True)
     label_piece = lax.all_gather(owners, "ctx", axis=0, tiled=True)
     scores = (
-        jnp.einsum("qhd,khd->hqk", queries, key_piece, preferred_element_type=jnp.float32) * factor
+        state_state(
+            keys_own,
+            "ctx",
+            0,
+            lambda part, at: jnp.einsum(
+                "qhd,khd->hqk", queries, part, preferred_element_type=jnp.float32
+            ),
+            2,
+        )
+        * factor
     )
     allowed = (owners[:, None] == label_piece[None, :]) & (owners[:, None] > 0)
     expo = jnp.where(allowed[None], jnp.exp(scores), 0.0)

time: 185 us -> 194 us (1.049)
  waiting for transfers between devices: 54.3 us -> 38.4 us
  local copies, waits for them, and re-layouts: 58.8 us -> 71.6 us
  starting transfers between devices: 11.9 us -> 16.4 us
  other arithmetic: 2.93 us -> 6.95 us
    ppermute x0 -> x3, waiting for transfers between devices: none -> 38.4 us  [the longest x1 20.4 us: state_state(): lax.ppermute(right_arr, axis_name, list(map(lambda i: (i, (i - 1) % mixed...]
    all_gather x1, waiting for transfers between devices: 32.6 us -> 0.02 us  [on_device(): value_piece = lax.all_gather(values_own, 'ctx', axis=0, tiled=True)]
    all_gather x1 -> x0, waiting for transfers between devices: 16.9 us -> none  [on_device(): key_piece = lax.all_gather(keys_own, 'ctx', axis=0, tiled=True)]
    concatenate x0 -> x1, local copies, waits for them, and re-layouts: none -> 12.8 us  [state_state(): jnp.roll(jnp.concatenate([*far_arr[::-1], *w2], axis=ndim_at), shift=(b_n...]
    ppermute x0 -> x3, starting transfers between devices: none -> 4.82 us  [the longest x2 2.42 us: state_state(): lax.ppermute(back, axis_name, list(map(lambda i: (i, (i + 1) % mixed_arr)...]
    reduce_sum x0 -> x1, other arithmetic: none -> 4.53 us  [on_device(): total = jnp.sum(expo, axis=-1).T]
    all_to_all x1, waiting for transfers between devices: 4.3 us -> 0.01 us  [on_device(): lax.all_to_all(out_labels, 'ctx', split_axis=0, concat_axis=0, tiled=True)]
    dot_general x1 -> x4, matrix products: 4.84 us -> 5 us  [on_device(): jnp.einsum('qhd,khd->hqk', queries, part, preferred_element_type=jnp.floa...]
  transfers between devices with their start and end apart: 5 -> 7, of which waited for: 4 -> 3; matrix products, arithmetic and copies ran while one was open for 32% -> 39% of each run, Pallas kernels for 0% -> 0%
where the time goes in v1:
time: 194 us; the launch traced here: 192 us
  local copies, waits for them, and re-layouts  71.6 us (37%)
  waiting for transfers between devices  38.4 us (20%)
  matrix products  35.2 us (18%)
  starting transfers between devices  16.4 us (8%)
  between operations  14.3 us (7%)
  blocking collectives  8.78 us (5%)
  other arithmetic  6.95 us (4%)
    unnamed x22, local copies, waits for them, and re-layouts  50.4 us
    ppermute x1, waiting for transfers between devices, state_state(): lax.ppermute(right_arr, axis_name, list(map(lambda i: (i, (i - 1) % mixed...  20.4 us
    dot_general x1, matrix products, on_device(): jnp.dot(normed, w_qkv.reshape(w_qkv.shape[0], -1), preferred_element_type...  18.8 us
    ppermute x2, waiting for transfers between devices, state_state(): lax.ppermute(back, axis_name, list(map(lambda i: (i, (i + 1) % mixed_arr)...  17.9 us
    concatenate x1, local copies, waits for them, and re-layouts, state_state(): jnp.roll(jnp.concatenate([*far_arr[::-1], *w2], axis=ndim_at), shift=(b_n...  12.8 us
    unnamed x1, blocking collectives  8.78 us
    all_to_all x1, starting transfers between devices, on_device(): lax.all_to_all(out_labels, 'ctx', split_axis=0, concat_axis=0, tiled=True)  5.89 us
    all_to_all x1, starting transfers between devices, on_device(): lax.all_to_all(outgoing, 'ctx', split_axis=0, concat_axis=0, tiled=True)  5.09 us
  transfers between devices with their start and end apart: 7, of which 3 were waited for; matrix products, arithmetic and copies ran while one was open for 39% of the time, Pallas kernels for 0%

profile of v1, /device:TPU:0, one launch (start us, length us, event | category | flops | bytes accessed | tf_op | source)
XLA Modules:
  0.0 191.5 jit_solution(10187147720428830437)
XLA Ops:
  6.5 1.2 slice_bitcast_fusion.2
  7.7 1.0 slice_bitcast_fusion.3
  8.7 0.8 concatenate.14
  9.6 1.6 fusion.31
  11.2 0.4 convolution_add_fusion.1
  11.7 1.8 convolution_convert_fusion
  13.5 0.1 copy.9
  13.6 0.1 reshape_reshape.3
  13.8 0.6 collective-permute-start
  14.3 0.1 fusion.38
  14.4 0.2 reduce_window_sum.11
  14.6 0.2 select_reduce_fusion
  14.8 1.0 scatter_custom_fusion.1
  15.8 0.7 all_to_all.10
  16.5 5.9 %all-to-all-start.1 = ((s32[4,1,48]{2,1,0:T(1,128)}), s32[4,1,48]{2,1,0:T(1,128)S(1)}, u32[]{:S(2)}, u32[]{:S(2)}) async-start(s32[4,1,48]{2,1,0:T(1,128)} %all_to_all.10), calls=%async_computation.1 | async-start | bytes 4096 | tf_op jit(solution)/shard_map/all_to_all | solution.py:100
  22.4 48.7 %copy.10 = bf16[6144,3,1024]{0,2,1:T(8,128)(2,1)} copy(bf16[6144,3,1024]{2,0,1:T(8,128)(2,1)} %param.15) | data formatting | bytes 75497472 | tf_op args[7]
  71.1 0.6 dynamic-slice.1
  72.3 0.5 broadcast.155
  72.8 0.7 reduce.3
  73.5 0.1 reshape.186
  73.6 0.9 scatter_custom_fusion
  74.5 0.7 reshape.205
  75.2 5.1 %all-to-all-start = ((bf16[4,2,1536]{2,1,0:T(2,128)(2,1)}), bf16[4,2,1536]{2,1,0:T(2,128)(2,1)S(1)}, u32[]{:S(2)}, u32[]{:S(2)}) async-start(bf16[4,2,1536]{2,1,0:T(2,128)(2,1)} %reshape.205), calls=%async_computation | async-start | bytes 49152 | tf_op jit(solution)/shard_map/all_to_all | solution.py:99
  80.3 0.2 dynamic-update-slice
  80.6 8.8 %all-reduce.2 = s32[768]{0:T(1024)S(1)} all-reduce(s32[768]{0:T(1024)S(1)} %dynamic-update-slice), channel_id=1, replica_groups=mesh['section'=2,'ctx'=4,'mp'=4] {'ctx'}, use_global_device_ids=true, to_apply=%add.2 | all-reduce | flops 768 | bytes 6144
  89.3 0.1 reshape.206
  89.5 2.9 %multiply_reduce_fusion = (f32[192]{0:T(256)S(1)}, f32[192,6144]{1,0:T(8,128)}) fusion(bf16[192,64]{1,0:T(8,128)(2,1)S(1)} %bitcast.96, bf16[64,6144]{1,0:T(8,128)(2,1)S(1)} %copy-done), kind=kOutput, calls=%fused_computation.4 | convolution fusion | flops 153354048 | bytes 5530368 | tf_op jit(solution)/shard_map/dot_general | solution.py:104
  92.4 18.8 %fusion.5 = f32[192,3,8,128]{3,0,2,1:T(8,128)S(1)} fusion(bf16[3,8,128,6144]{3,2,1,0:T(8,128)(2,1)} %bitcast.92, f32[192,6144]{1,0:T(8,128)} %get-tuple-element.12, f32[6144]{0:T(1024)S(1)} %copy-done.5, f32[192]{0:T(256)S(1)} %add_rsqrt_fusion.2), kind=kOutput, calls=%fused_computation.9 | convolution fusion | flops 7251296256 | bytes 44851968 | tf_op jit(solution)/shard_map/dot_general | solution.py:109
  111.2 0.6 multiply_reduce_fusion.1
  111.8 0.8 slice.70
  112.6 0.5 multiply_convert_fusion.2
  113.1 1.5 collective-permute-start.1
  114.6 0.2 compare_and_fusion
  114.8 2.4 %collective-permute-start.3 = (bf16[192,8,128]{2,0,1:T(8,128)(2,1)S(1)}, bf16[192,8,128]{2,0,1:T(8,128)(2,1)S(1)}, u32[]{:S(2)}, u32[]{:S(2)}) collective-permute-start(bf16[192,8,128]{2,0,1:T(8,128)(2,1)S(1)} %get-tuple-element.7), channel_id=1, source_target_pairs={{0,12},{4,0},{8,4},{12,8},{1,13},{5,1},{9,5},{13,9},{2,14},{6,2},{... | collective-permute-start | bytes 1179656 | tf_op jit(solution)/shard_map/ppermute | solution.py:25
  117.2 0.4 fusion.55
  117.6 12.2 %collective-permute-done.1 = bf16[192,8,128]{2,0,1:T(8,128)(2,1)S(1)} collective-permute-done((bf16[192,8,128]{2,0,1:T(8,128)(2,1)S(1)}, bf16[192,8,128]{2,0,1:T(8,128)(2,1)S(1)}, u32[]{:S(2)}, u32[]{:S(2)}) %collective-permute-start.1) | collective-permute-done | bytes 393248 | tf_op jit(solution)/shard_map/ppermute | solution.py:22
  129.8 0.9 collective-permute-start.2
  130.7 1.6 fusion.54
  132.3 20.4 %collective-permute-done.3 = bf16[192,8,128]{2,0,1:T(8,128)(2,1)S(1)} collective-permute-done((bf16[192,8,128]{2,0,1:T(8,128)(2,1)S(1)}, bf16[192,8,128]{2,0,1:T(8,128)(2,1)S(1)}, u32[]{:S(2)}, u32[]{:S(2)}) %collective-permute-start.3) | collective-permute-done | bytes 393248 | tf_op jit(solution)/shard_map/ppermute | solution.py:25
  152.7 1.5 fusion.56
  154.3 5.7 %collective-permute-done.2 = bf16[192,8,128]{2,0,1:T(8,128)(2,1)S(1)} collective-permute-done((bf16[192,8,128]{2,0,1:T(8,128)(2,1)S(1)}, bf16[192,8,128]{2,0,1:T(8,128)(2,1)S(1)}, u32[]{:S(2)}, u32[]{:S(2)}) %collective-permute-start.2) | collective-permute-done | bytes 393248 | tf_op jit(solution)/shard_map/ppermute | solution.py:22
  160.0 1.5 fusion.53
  161.5 12.8 %concatenate.15 = f32[8,192,1536]{2,1,0:T(8,128)} concatenate(f32[8,192,192]{2,1,0:T(8,128)} %fusion.53, f32[8,192,192]{2,1,0:T(8,128)} %fusion.54, f32[8,192,192]{2,1,0:T(8,128)S(1)} %fusion.55, f32[8,192,192]{2,1,0:T(8,128)} %fusion.56, f32[8,192,192]{2,1,0:T(8,128)} %fusion.53, f32[8,192,192]{2,1,0:T(8,128)} %fusion.54, f32[8,192,192]{2,1,0:T(8,128)S(1)} %fusion.55, ...), dimensions={2} | concatenate | bytes 18874368 | tf_op jit(solution)/shard_map/jit(_roll_dynamic)/concatenate | solution.py:28
  174.3 4.5 %fusion = f32[8,192]{1,0:T(8,128)S(1)} fusion(f32[8,192,1536]{2,1,0:T(8,128)} %concatenate.15, s32[]{:T(128)S(6)} %select_n.42, pred[192,768]{1,0:T(8,128)(4,1)S(1)} %compare_and_fusion), kind=kLoop, calls=%fused_computation.5 | loop fusion | flops 3537408 | bytes 4872196 | tf_op jit(solution)/shard_map/reduce_sum | solution.py:133
  178.8 0.0 all-gather.3.cloned.1.call-done
  178.9 4.6 %fusion.23 = bf16[192,8,128]{2,0,1:T(8,128)(2,1)S(1)} fusion(bf16[768,1,8,128]{3,0,2,1:T(8,128)(2,1)} %all-gather.3.cloned.1.call-done, f32[8,192,1536]{2,1,0:T(8,128)} %concatenate.15, s32[]{:T(128)S(6)} %select_n.42, pred[192,768]{1,0:T(8,128)(4,1)S(1)} %compare_and_fusion, f32[192,8]{0,1:T(8,128)S(1)} %add_bitcast_fusion), kind=kOutput, calls=%fused_computation.22 | convolution fusion | flops 305922048 | bytes 6838276 | tf_op jit(solution)/shard_map/hqk,khd->qhd/dot_general | solution.py:134
  183.5 0.3 copy.11
  183.8 0.9 convert_element_type.66
  (30 shorter events, 0.2 us)
Async XLA Ops:
  6.5 82.9 %copy-start = (bf16[64,6144]{1,0:T(8,128)(2,1)S(1)}, bf16[64,6144]{1,0:T(8,128)(2,1)}, u32[]{:S(2)}) copy-start(bf16[64,6144]{1,0:T(8,128)(2,1)} %param.13) | copy-start | bytes 2359300
  6.5 4.7 %copy-start.2 = (bf16[3,512,512]{2,1,0:T(8,128)(2,1)S(1)}, bf16[3,512,512]{2,1,0:T(8,128)(2,1)}, u32[]{:S(2)}) copy-start(bf16[3,512,512]{2,1,0:T(8,128)(2,1)} %param.9) | copy-start | bytes 4718596
  6.5 5.1 %copy-start.6 = (bf16[512,16]{0,1:T(8,128)(2,1)S(1)}, bf16[512,16]{0,1:T(8,128)(2,1)}, u32[]{:S(2)}) copy-start(bf16[512,16]{0,1:T(8,128)(2,1)} %param.10) | copy-start | bytes 49156
  11.2 3.1 %copy-start.3 = (s32[2,128,1]{1,2,0:T(1,128)S(1)}, s32[2,128,1]{1,2,0:T(1,128)}, u32[]{:S(2)}) copy-start(s32[2,128,1]{1,2,0:T(1,128)} %param.11) | copy-start | bytes 3076
  11.2 3.6 %copy-start.4 = (s32[2,128]{1,0:T(2,128)S(1)}, s32[2,128]{1,0:T(2,128)}, u32[]{:S(2)}) copy-start(s32[2,128]{1,0:T(2,128)} %param.12) | copy-start | bytes 3076
  13.8 59.8 %collective-permute-start = (bf16[128,64]{1,0:T(8,128)(2,1)S(1)}, bf16[128,64]{1,0:T(8,128)(2,1)S(1)}, u32[]{:S(2)}, u32[]{:S(2)}) collective-permute-start(bf16[128,64]{1,0:T(8,128)(2,1)S(1)} %reshape_reshape.3), channel_id=1, source_target_pairs={{0,16},{16,0},{1,17},{17,1},{2,18},{18,2},{3,19},{19,3},{4,20},{20... | collective-permute-start | bytes 49160 | tf_op jit(solution)/shard_map/ppermute | solution.py:43
  16.5 55.9 %all-to-all-start.1 = ((s32[4,1,48]{2,1,0:T(1,128)}), s32[4,1,48]{2,1,0:T(1,128)S(1)}, u32[]{:S(2)}, u32[]{:S(2)}) async-start(s32[4,1,48]{2,1,0:T(1,128)} %all_to_all.10), calls=%async_computation.1 | async-start | bytes 4096 | tf_op jit(solution)/shard_map/all_to_all | solution.py:100
  22.4 48.7 %copy-start.7 = (u32[32]{0:T(128)S(1)}, u32[32]{0:T(128)}, u32[]{:S(2)}) copy-start(u32[32]{0:T(128)} %constant.103) | copy-start | bytes 388
  71.1 21.3 %copy-start.5 = (f32[6144]{0:T(1024)S(1)}, f32[6144]{0:T(1024)}, u32[]{:S(2)}) copy-start(f32[6144]{0:T(1024)} %param.14) | copy-start | bytes 73732
  75.2 14.1 %all-to-all-start = ((bf16[4,2,1536]{2,1,0:T(2,128)(2,1)}), bf16[4,2,1536]{2,1,0:T(2,128)(2,1)S(1)}, u32[]{:S(2)}, u32[]{:S(2)}) async-start(bf16[4,2,1536]{2,1,0:T(2,128)(2,1)} %reshape.205), calls=%async_computation | async-start | bytes 49152 | tf_op jit(solution)/shard_map/all_to_all | solution.py:99
  80.3 98.6 %all-gather.3.cloned.1.call-start = ((), (), s32[]{:S(2)}) async-start(), calls=%async_computation.2 | async-start | bytes 1966080 | tf_op jit(solution)/shard_map/all_gather | solution.py:117
  113.1 16.7 %collective-permute-start.1 = (bf16[192,8,128]{2,0,1:T(8,128)(2,1)S(1)}, bf16[192,8,128]{2,0,1:T(8,128)(2,1)S(1)}, u32[]{:S(2)}, u32[]{:S(2)}) collective-permute-start(bf16[192,8,128]{2,0,1:T(8,128)(2,1)S(1)} %get-tuple-element.7), channel_id=1, source_target_pairs={{0,4},{4,8},{8,12},{12,0},{1,5},{5,9},{9,13},{13,1},{2,6},{6,10},{... | collective-permute-start | bytes 1179656 | tf_op jit(solution)/shard_map/ppermute | solution.py:22
  114.8 37.9 %collective-permute-start.3 = (bf16[192,8,128]{2,0,1:T(8,128)(2,1)S(1)}, bf16[192,8,128]{2,0,1:T(8,128)(2,1)S(1)}, u32[]{:S(2)}, u32[]{:S(2)}) collective-permute-start(bf16[192,8,128]{2,0,1:T(8,128)(2,1)S(1)} %get-tuple-element.7), channel_id=1, source_target_pairs={{0,12},{4,0},{8,4},{12,8},{1,13},{5,1},{9,5},{13,9},{2,14},{6,2},{... | collective-permute-start | bytes 1179656 | tf_op jit(solution)/shard_map/ppermute | solution.py:25
  129.8 30.1 %collective-permute-start.2 = (bf16[192,8,128]{2,0,1:T(8,128)(2,1)S(1)}, bf16[192,8,128]{2,0,1:T(8,128)(2,1)S(1)}, u32[]{:S(2)}, u32[]{:S(2)}) collective-permute-start(bf16[192,8,128]{2,0,1:T(8,128)(2,1)S(1)} %collective-permute-done.1), channel_id=1, source_target_pairs={{0,4},{4,8},{8,12},{12,0},{1,5},{5,9},{9,13},{13,1},{2,6},{6,10},{... | collective-permute-start | bytes 1179656 | tf_op jit(solution)/shard_map/ppermute | solution.py:22
  178.8 5.9 %copy-start.1 = (bf16[64,6144]{1,0:T(8,128)(2,1)S(1)}, bf16[64,6144]{1,0:T(8,128)(2,1)}, u32[]{:S(2)}) copy-start(bf16[64,6144]{1,0:T(8,128)(2,1)} %param.13) | copy-start | bytes 2359300
Sparse Core Ops, SparseCore 0:
  112.7 52.6 all-gather.2
